TPU v7x, 32 devices: a whole 2x2x4 slice. The times are simulated.
32 devices in a mesh: outer: 4 (over y, x), inner: 8 (over z, core).
Axes of the slice: x: 2, y: 2, z: 4, core: 2. Of those that a mesh axis runs over, the one named last changes fastest.
Arguments:
- queries: bfloat16 [8192, 1024], P(('outer', 'inner')), may hold values from -6 to 6
- keys: bfloat16 [2, 8192, 1024], P(None, ('outer', 'inner')), may hold values from -6 to 6
- values: bfloat16 [2, 8192, 1024], P(None, ('outer', 'inner')), may hold values from -6 to 6
- betas: float32 [2, 8, 8192], P(None, None, ('outer', 'inner')), may hold values from 0 to 2
- log_decay: float32 [8, 8192], P(None, ('outer', 'inner')), may hold values from -1 to 0
- out_gain: float32 [128], replicated, may hold values from 0.5 to 1.5
Outputs:
- mixed: bfloat16 [8192, 1024], P(('outer', 'inner'))
All inputs are finite; a program needn't handle non-finite values.
Results may differ from a plain program's by a relative error of at most 0.0018.
Values sent between devices are 32-bit elements; how exact they have to be, the bound alone decides.
A program may use at most 128 MiB of HBM per device.

v0:
```python
import jax
import jax.numpy as jnp
from jax import lax
from jax.sharding import PartitionSpec as P

BLOCK_LEN = 64


HIGHEST = lax.Precision.HIGHEST


def entering(part, axis, combine, identity):
    place = lax.axis_index(axis)
    gathered = jax.tree.map(lambda a: lax.all_gather(a, axis), part)
    state = jax.tree.map(lambda a, e: jnp.zeros_like(a) + jnp.asarray(e, a.dtype), part, identity)

    def one(hop, state):
        return combine(
            state, jax.tree.map(lambda a: lax.dynamic_index_in_dim(a, hop, 0, False), gathered)
        )

    return lax.fori_loop(0, place, one, state)


def spread(x, axis, root):
    mine = lax.axis_index(axis) == root
    return lax.psum(jnp.where(mine, x, jnp.zeros_like(x)), axis)


def prepare(queries, keys, values, betas, log_decay, span):
    length = queries.shape[0]
    heads = betas.shape[1]
    width_k = queries.shape[1] // heads
    width_v = values.shape[2] // heads
    blocks = length // span
    reflect = 2 * span
    query_b = queries.reshape(blocks, span, heads, width_k).transpose(0, 2, 1, 3)
    query_f = query_b.astype(jnp.float32)
    query_inv = lax.rsqrt(jnp.sum(query_f * query_f, -1) + 1e-06)
    query_n = query_f * query_inv[..., None]
    key_b = (
        keys.reshape(2, blocks, span, heads, width_k)
        .transpose(1, 3, 2, 0, 4)
        .reshape(blocks, heads, reflect, width_k)
    )
    key_f = key_b.astype(jnp.float32)
    key_inv = lax.rsqrt(jnp.sum(key_f * key_f, -1) + 1e-06)
    key_n = key_f * key_inv[..., None]
    value_n = (
        values.astype(jnp.float32).reshape(2, blocks, span, heads, width_v).transpose(1, 3, 2, 0, 4)
    )
    value_n = value_n.reshape(blocks, heads, reflect, width_v)
    beta_r = (
        betas.reshape(2, heads, blocks, span).transpose(2, 1, 3, 0).reshape(blocks, heads, reflect)
    )
    decay_t = log_decay.reshape(heads, blocks, span).transpose(1, 0, 2)
    decay_r = jnp.stack([decay_t, jnp.zeros_like(decay_t)], -1).reshape(blocks, heads, reflect)
    cumulative = jnp.cumsum(decay_r, -1)
    row_idx = lax.broadcasted_iota(jnp.int32, (reflect, reflect), 0)
    col_idx = lax.broadcasted_iota(jnp.int32, (reflect, reflect), 1)
    key_gram = (
        jnp.einsum("nhrd,nhsd->nhrs", key_b, key_b, preferred_element_type=jnp.float32)
        * key_inv[..., :, None]
        * key_inv[..., None, :]
    )
    fall_off = jnp.exp(jnp.minimum(cumulative[..., :, None] - cumulative[..., None, :], 0.0))
    strict_low = jnp.where(row_idx > col_idx, key_gram * fall_off, 0.0)
    system = jnp.eye(reflect, dtype=jnp.float32) + beta_r[..., :, None] * strict_low
    scaled = jnp.exp(cumulative)
    right_side = jnp.concatenate(
        [(beta_r * scaled)[..., None] * key_n, beta_r[..., None] * value_n], -1
    )
    solved = lax.linalg.triangular_solve(
        system, right_side, left_side=True, lower=True, unit_diagonal=True
    )
    write_key = solved[..., :width_k]
    write_val = solved[..., width_k:]
    tok_idx = lax.broadcasted_iota(jnp.int32, (span, reflect), 0)
    ref_idx = lax.broadcasted_iota(jnp.int32, (span, reflect), 1)
    query_cum = cumulative.reshape(blocks, heads, span, 2)[..., 1]
    query_key = (
        jnp.einsum("nhcd,nhsd->nhcs", query_b, key_b, preferred_element_type=jnp.float32)
        * query_inv[..., :, None]
        * key_inv[..., None, :]
    )
    fade = jnp.exp(jnp.minimum(query_cum[..., :, None] - cumulative[..., None, :], 0.0))
    reach = jnp.where(ref_idx <= 2 * tok_idx + 1, query_key * fade, 0.0)
    reduced = jnp.exp(query_cum)[..., None] * query_n - jnp.einsum(
        "nhcs,nhsd->nhcd", reach, write_key, precision=HIGHEST
    )
    local_out = jnp.einsum("nhcs,nhsd->nhcd", reach, write_val, precision=HIGHEST)
    last_cum = cumulative[..., -1:]
    tail = jnp.exp(last_cum - cumulative)
    trans = jnp.exp(last_cum)[..., None] * jnp.eye(width_k, dtype=jnp.float32)
    trans = trans - jnp.einsum(
        "nhsd,nhse->nhde", tail[..., None] * write_key, key_n, precision=HIGHEST
    )
    inject = jnp.einsum("nhsd,nhse->nhde", tail[..., None] * write_val, key_n, precision=HIGHEST)
    return (reduced, local_out, trans, inject)


def compose(earlier, later):
    new_map = jnp.einsum("hde,hef->hdf", earlier[0], later[0], precision=HIGHEST)
    new_add = jnp.einsum("hde,hef->hdf", earlier[1], later[0], precision=HIGHEST) + later[1]
    return (new_map, new_add)


def advance(state_pair, inputs):
    prefix_map, prefix_add = state_pair
    red_b, loc_b, trans_b, inj_b = inputs
    carried = jnp.einsum("hcd,hed->hce", red_b, prefix_map, precision=HIGHEST)
    base_out = jnp.einsum("hcd,hed->hce", red_b, prefix_add, precision=HIGHEST) + loc_b
    next_pair = compose((prefix_map, prefix_add), (trans_b, inj_b))
    return (next_pair, (carried, base_out))


def per_device(queries, keys, values, betas, log_decay, out_gain):
    heads = betas.shape[1]
    width_k = queries.shape[1] // heads
    width_v = values.shape[2] // heads
    reduced, local_out, trans, inject = prepare(queries, keys, values, betas, log_decay, BLOCK_LEN)
    identity = (
        jnp.broadcast_to(jnp.eye(width_k, dtype=jnp.float32), (heads, width_k, width_k)),
        jnp.zeros((heads, width_v, width_k), jnp.float32),
    )
    own_pair, pieces = lax.scan(advance, identity, (reduced, local_out, trans, inject))
    carried, base_out = pieces
    before_map, before_add = entering(own_pair, "inner", compose, identity)
    through = compose((before_map, before_add), own_pair)
    group_map, group_add = (
        spread(through[0], "inner", lax.axis_size("inner") - 1),
        spread(through[1], "inner", lax.axis_size("inner") - 1),
    )
    group_state = entering((group_map, group_add), "outer", compose, identity)[1]
    entering_state = (
        jnp.einsum("hde,hef->hdf", group_state, before_map, precision=HIGHEST) + before_add
    )
    readout = jnp.einsum("nhcd,hed->nhce", carried, entering_state, precision=HIGHEST) + base_out
    mean_sq = jnp.mean(readout * readout, -1, keepdims=True)
    normed = readout * lax.rsqrt(mean_sq + 1e-05) * out_gain
    blocks = normed.shape[0]
    return (
        normed.transpose(0, 2, 1, 3)
        .reshape(blocks * BLOCK_LEN, heads * width_v)
        .astype(jnp.bfloat16)
    )


def solution(mesh):
    placed = (
        P(("outer", "inner"), None),
        P(None, ("outer", "inner"), None),
        P(None, ("outer", "inner"), None),
        P(None, None, ("outer", "inner")),
        P(None, ("outer", "inner")),
        P(),
    )
    return jax.shard_map(
        per_device,
        mesh=mesh,
        in_specs=placed,
        out_specs=P(("outer", "inner"), None),
        check_vma=False,
    )
```

profile of v0, /device:TPU:13, one launch (start us, length us, event | category | flops | bytes accessed | tf_op | source)
XLA Modules:
  0.0 687.0 jit_solution(12705137376245005066)
XLA Ops:
  6.5 1.5 copy.206
  8.0 2.3 multiply_reduce_fusion
  10.3 1.1 copy.136
  11.8 1.1 reduce_window_sum.11
  14.4 3.4 add_bitcast_fusion
  17.8 315.9 %custom-call.3 = f32[4,8,1,128,128]{3,4,2,1,0:T(8,128)} custom-call(f32[4,8,1,128,128]{4,3,2,1,0:T(8,128)} %add_bitcast_fusion), custom_call_target="InvertDiagBlocksLowerTriangular" | custom-call | tf_op jit(solution)/shard_map/triangular_solve | solution.py:73
  333.8 2.2 fusion.44
  336.3 1.6 copy.142
  337.9 1.9 broadcast_multiply_fusion
  340.8 6.6 fusion.35
  348.3 3.0 fusion.45
  351.2 3.0 fusion.53
  354.3 6.0 fusion.40
  360.3 6.2 multiply_subtract_fusion
  366.6 31.3 %while.43 = (s32[]{:T(128)}, f32[8,128,128]{1,2,0:T(8,128)S(1)}, f32[8,128,128]{1,2,0:T(8,128)S(1)}, f32[4,8,64,128]{3,2,0,1:T(8,128)}, f32[4,8,64,128]{3,2,0,1:...) while((s32[]{:T(128)}, f32[8,128,128]{1,2,0:T(8,128)S(1)}, ...), condition=%wide.region_4.5_spmd.clone, body=%wide.region_3.4_spmd.clone.sunk | while | flops 604438528 | bytes 8129660 | solution.py:126
  366.6 2.3 fusion.131
  369.0 2.1 fusion.129
  371.1 2.3 fusion.130
  374.5 2.3 fusion.131
  376.8 2.1 fusion.129
  378.9 2.3 fusion.130
  382.3 2.3 fusion.131
  384.6 2.1 fusion.129
  386.7 2.3 fusion.130
  390.1 2.3 fusion.131
  392.4 2.1 fusion.129
  394.5 2.3 fusion.130
  400.0 46.2 %all-gather.11.cloned.1.call-done = f32[64,128,128]{2,1,0:T(8,128)} async-done(((f32[8,128,128]{2,1,0:T(8,128)}), f32[64,128,128]{2,1,0:T(8,128)}) %all-gather.11.cloned.1.call-update) | async-done | bytes 4194320 | tf_op jit(solution)/shard_map/all_gather | solution.py:14
  446.2 47.3 %all-gather.13.cloned.1.call-done = f32[64,128,128]{2,1,0:T(8,128)} async-done(((f32[8,128,128]{2,1,0:T(8,128)}), f32[64,128,128]{2,1,0:T(8,128)}) %all-gather.13.cloned.1.call-update) | async-done | bytes 4194320 | tf_op jit(solution)/shard_map/all_gather | solution.py:14
  493.6 16.7 %while.41 = (s32[]{:T(128)}, f32[8,128,128]{1,2,0:T(8,128)S(1)}, f32[8,128,128]{1,2,0:T(8,128)S(1)}, s32[]{:T(128)}, f32[8,8,128,128]{3,2,1,0:T(8,128)}, /*index...) while((s32[]{:T(128)}, f32[8,128,128]{1,2,0:T(8,128)S(1)}, f32[8,128,128]{1,2,0:T(8,128)S(1)}, ...), condition=%wide.region_6.7_spmd, body=%wide.region_5.6_spmd.sunk | while | flops 402784256 | bytes 7864459 | solution.py:22
  493.6 1.1 constant_dynamic-slice_fusion.4
  495.0 2.1 fusion.117
  497.1 2.1 convolution_bitcast_fusion.9
  499.2 1.1 constant_dynamic-slice_fusion.4
  500.6 2.1 fusion.117
  502.7 2.1 convolution_bitcast_fusion.9
  506.1 2.1 fusion.117
  508.2 2.1 convolution_bitcast_fusion.9
  510.3 1.9 fusion.63
  512.2 1.8 fusion.60
  514.1 78.8 %all-reduce.4.cloned.1.call-done = (f32[1,8,128,128]{3,2,1,0:T(8,128)}, f32[1,8,128,128]{3,2,1,0:T(8,128)}) async-done(((f32[1,8,128,128]{3,2,1,0:T(8,128)}, f32[1,8,128,128]{3,2,1,0:T(8,128)}), (f32[1,8,128,128]{3,2,1,0:T(8,128)}, f32[1,8,128,128]{3,2,1,0:T(8,128)})) %all-reduce.4.cloned.1.call-update) | async-done | bytes 1048592 | tf_op jit(solution)/shard_map/psum | solution.py:27
  593.7 37.3 %all-gather.7.cloned.1.call-done = f32[4,8,128,128]{3,2,1,0:T(8,128)} async-done(((f32[1,8,128,128]{3,2,1,0:T(8,128)}), f32[4,8,128,128]{3,2,1,0:T(8,128)}) %all-gather.7.cloned.1.call-update) | async-done | bytes 2097168 | tf_op jit(solution)/shard_map/all_gather | solution.py:14
  631.0 36.9 %all-gather.9.cloned.1.call-done = f32[4,8,128,128]{3,2,1,0:T(8,128)} async-done(((f32[1,8,128,128]{3,2,1,0:T(8,128)}), f32[4,8,128,128]{3,2,1,0:T(8,128)}) %all-gather.9.cloned.1.call-update) | async-done | bytes 2097168 | tf_op jit(solution)/shard_map/all_gather | solution.py:14
  668.0 7.1 %while.42 = (s32[]{:T(128)}, f32[8,128,128]{1,2,0:T(8,128)S(1)}, s32[]{:T(128)}, f32[4,8,128,128]{3,2,1,0:T(8,128)}, f32[4,8,128,128]{3,2,1,0:T(8,128)}, /*index=5*/s32[]{:T(128)}, s32[]{:T(128)}, s32[]{:T(128)}) while((s32[]{:T(128)}, f32[8,128,128]{1,2,0:T(8,128)S(1)}, s32[]{:T(128)}, f32[4,8,128,128]{3,2,1,0:T(8,128)}, ...), condition=%wide.region_10.11_spmd, body=%wide.region_9.10_spmd.sunk | while | flops 201457664 | bytes 5243007 | solution.py:22
  668.0 1.1 constant_dynamic-slice_fusion.5
  669.3 2.1 fusion.120
  672.8 2.1 fusion.120
  676.3 2.5 multiply_reduce_fusion.1
  (94 shorter events, 17.6 us)
Async XLA Ops:
  6.5 439.7 %all-gather.11.cloned.1.call-start = ((), (), s32[]{:S(2)}) async-start(), calls=%async_computation.2 | async-start | bytes 4718592 | tf_op jit(solution)/shard_map/all_gather | solution.py:14
  8.0 3.4 copy-start.6
  10.3 3.6 copy-start.5
  11.4 342.8 %copy-start = (bf16[2,4,64,8,128]{4,0,2,3,1:T(2,128)(2,1)}, bf16[2,4,64,8,128]{4,0,2,3,1:T(2,128)(2,1)S(1)}, u32[]{:S(2)}) copy-start(bf16[2,4,64,8,128]{4,0,2,3,1:T(2,128)(2,1)S(1)} %copy.136) | copy-start | bytes 3145732
  17.8 318.2 %copy-start.2 = (bf16[2,256,1024]{2,1,0:T(8,128)(2,1)S(1)}, bf16[2,256,1024]{2,1,0:T(8,128)(2,1)}, u32[]{:S(2)}) copy-start(bf16[2,256,1024]{2,1,0:T(8,128)(2,1)} %param.14) | copy-start | bytes 3145732
  337.9 2.2 copy-start.4
  398.9 94.6 %all-gather.13.cloned.1.call-start = ((), (), s32[]{:S(2)}) async-start(), calls=%async_computation.3 | async-start | bytes 4718592 | tf_op jit(solution)/shard_map/all_gather | solution.py:14
  400.0 192.9 %all-reduce.4.cloned.1.call-start = ((), (), s32[]{:S(2)}) async-start(), calls=%async_computation.4 | async-start | bytes 2097152 | tf_op jit(solution)/shard_map/psum | solution.py:27
  493.6 16.7 %copy-start.1 = (f32[8,128,128]{2,1,0:T(8,128)S(1)}, f32[8,128,128]{2,1,0:T(8,128)}, u32[]{:S(2)}) copy-start(f32[8,128,128]{2,1,0:T(8,128)} %copy.154) | copy-start | bytes 1572868
  514.0 117.0 %all-gather.7.cloned.1.call-start = ((), (), s32[]{:S(2)}) async-start(), calls=%async_computation | async-start | bytes 2621440 | tf_op jit(solution)/shard_map/all_gather | solution.py:14
  592.9 75.0 %all-gather.9.cloned.1.call-start = ((), (), s32[]{:S(2)}) async-start(), calls=%async_computation.1 | async-start | bytes 2621440 | tf_op jit(solution)/shard_map/all_gather | solution.py:14
  675.1 1.2 copy-start.3
  676.1 2.7 copy-start.7
Sparse Core Ops, SparseCore 0:
  399.0 47.1 all-gather.10
  447.8 45.6 all-gather.12
  514.1 78.7 all-reduce.3
  594.6 36.4 all-gather.6
  632.7 35.1 all-gather.8
where the time goes:
time: 692 us; the launch traced here: 687 us
  other arithmetic  324 us (47%)
  waiting for transfers between devices  247 us (36%)
  matrix products  83.6 us (12%)
  local copies, waits for them, and re-layouts  17.3 us (2%)
  between operations  13.5 us (2%)
    another operation x2, other arithmetic, prepare(): lax.linalg.triangular_solve(system, right_side, left_side=True, lower=Tru...  316 us
    all_gather x4, waiting for transfers between devices, entering(): gathered = jax.tree.map(lambda a: lax.all_gather(a, axis), part)  168 us
    psum x1, waiting for transfers between devices, spread(): return lax.psum(jnp.where(mine, x, jnp.zeros_like(x)), axis)  78.8 us
    dot_general x10, matrix products, compose(): jnp.einsum('hde,hef->hdf', earlier[1], later[0], precision=HIGHEST)  20.4 us
  transfers between devices with their start and end apart: 5, of which 5 were waited for; matrix products, arithmetic and copies ran while one was open for 0% of the time, Pallas kernels for 0%

commit v1 on v0

v1 whole, which is shorter than its diff:
```python
import functools

import jax
import jax.numpy as jnp
from jax import lax
from jax.experimental import pallas as pl
from jax.experimental.pallas import tpu as pltpu
from jax.sharding import PartitionSpec as P

BLOCK_LEN = 64
F32 = jnp.float32
BF16 = jnp.bfloat16


def split(x):
    high = x.astype(BF16)
    low = (x - high.astype(F32)).astype(BF16)
    return high, low


def dot(a, b):
    return lax.dot_general(a, b, (((1,), (0,)), ((), ())), preferred_element_type=F32)


def dot_t(a, b):
    return lax.dot_general(a, b, (((1,), (1,)), ((), ())), preferred_element_type=F32)


def wide(x):
    return jnp.concatenate(split(x), 1)


def mul(a, b):
    a2 = wide(a)
    bh, bl = split(b)
    if b.shape[1] == 128:
        row = jnp.concatenate([bh, bl], 1)
        both = dot(a2, jnp.concatenate([row, row], 0))
        return both[:, :128] + both[:, 128:]
    return dot(a2, jnp.concatenate([bh, bh], 0)) + dot(a2[:, :128], bl)


def mul_left(a, b):
    return dot(wide(a), jnp.concatenate([b, b], 0))


def add_right(x, y):
    return jnp.concatenate([x[:, :128], x[:, 128:] + y], 1)


def local_kernel(blocks, q_ref, k_ref, v_ref, s_ref, x_ref, c_ref, b_ref):
    span = BLOCK_LEN
    size = 2 * span
    row = lax.broadcasted_iota(jnp.int32, (size, size), 0)
    col = lax.broadcasted_iota(jnp.int32, (size, size), 1)
    row_t, col_t = row % span, col % span
    row_rank, col_rank = 2 * row_t + row // span, 2 * col_t + col // span
    eye = row == col
    eye_f = eye.astype(F32)
    lower = row_rank > col_rank
    c_mask = (col_t <= row_t) & (col < span)
    r_mask = (row_t <= col_t) & (row < span)
    levels = []
    width = 1
    while width < size:
        levels.append(
            (row_rank // (2 * width) == col_rank // (2 * width))
            & (row_rank // width != col_rank // width)
            & lower
        )
        width *= 2

    work = []
    for n in range(blocks):
        at = pl.ds(n * span, span)
        q_b = q_ref[at, :]
        k_b = jnp.concatenate([k_ref[0, at, :], k_ref[1, at, :]], 0)
        v_b = jnp.concatenate([v_ref[0, at, :], v_ref[1, at, :]], 0)
        d_row = s_ref[0, n : n + 1, :]
        beta_row = s_ref[0, blocks + n : blocks + n + 1, :]
        d_col = jnp.sum(jnp.where(eye, d_row, 0.0), 1, keepdims=True)
        beta_col = jnp.sum(jnp.where(eye, beta_row, 0.0), 1, keepdims=True)
        c_col = jnp.sum(jnp.where(c_mask, d_row, 0.0), 1, keepdims=True)
        c_row = jnp.sum(jnp.where(r_mask, d_col, 0.0), 0, keepdims=True)
        gram = dot_t(k_b, k_b)
        k_f = k_b.astype(F32)
        q_f = q_b.astype(F32)
        ki_col = lax.rsqrt(jnp.sum(k_f * k_f, 1, keepdims=True) + 1e-06)
        ki_row = lax.rsqrt(jnp.sum(jnp.where(eye, gram, 0.0), 0, keepdims=True) + 1e-06)
        qi_col = lax.rsqrt(jnp.sum(q_f * q_f, 1, keepdims=True) + 1e-06)
        fall = jnp.exp(jnp.minimum(c_col - c_row, 0.0))
        low = jnp.where(lower, gram * (beta_col * ki_col) * ki_row * fall, 0.0)
        reach = dot_t(q_b, k_b) * qi_col * ki_row * fall[:span]
        reach = jnp.where(col_t[:span] <= row_t[:span], reach, 0.0)
        query = q_f * (qi_col * jnp.exp(c_col[:span]))
        work.append((k_b, v_b, beta_row, c_row, c_col, ki_row, ki_col, low, reach, query))

    inverse = [eye_f - jnp.where(levels[0], w[7], 0.0) for w in work]
    for mask in levels[1:]:
        part = [mul(jnp.where(mask, w[7], 0.0), t) for w, t in zip(work, inverse)]
        inverse = [t - mul(t, p) for t, p in zip(inverse, part)]

    state = None
    for n in range(blocks):
        k_b, v_b, beta_row, c_row, c_col, ki_row, ki_col, low, reach, query = work[n]
        t = inverse[n] * beta_row
        written = jnp.concatenate(
            [mul_left(t * (ki_row * jnp.exp(c_row)), k_b), mul_left(t, v_b)], 1
        )
        got = mul(reach, written)
        reduced, local_out = query - got[:, :128], got[:, 128:]
        last = c_col[span - 1 : span, :]
        tail = jnp.exp(last - c_col) * ki_col
        wh, wl = split(written * tail)
        k_t = jnp.transpose(k_b.astype(F32)).astype(BF16)
        made = dot(jnp.concatenate([k_t, k_t], 1), jnp.concatenate([wh, wl], 0))
        trans = jnp.exp(last) * eye_f - made[:, :128]
        inject = made[:, 128:]
        at = pl.ds(n * span, span)
        if state is None:
            c_ref[0, at, :] = reduced
            b_ref[0, at, :] = local_out
            state = jnp.concatenate([trans, inject], 1)
        else:
            read = mul(reduced, state)
            c_ref[0, at, :] = read[:, :128]
            b_ref[0, at, :] = read[:, 128:] + local_out
            state = add_right(mul(trans, state), inject)
    x_ref[0] = state


def local_phase(queries, keys, values, betas, log_decay):
    length = queries.shape[0]
    heads = betas.shape[1]
    blocks = length // BLOCK_LEN
    beta = betas.reshape(2, heads, blocks, BLOCK_LEN).transpose(1, 2, 0, 3)
    beta = beta.reshape(heads, blocks, 2 * BLOCK_LEN)
    decay = log_decay.reshape(heads, blocks, 1, BLOCK_LEN)
    decay = jnp.concatenate([decay, decay], 2).reshape(heads, blocks, 2 * BLOCK_LEN)
    small = jnp.concatenate([decay, beta], 1)
    return pl.pallas_call(
        functools.partial(local_kernel, blocks),
        grid=(heads,),
        in_specs=[
            pl.BlockSpec((length, 128), lambda h: (0, h)),
            pl.BlockSpec((2, length, 128), lambda h: (0, 0, h)),
            pl.BlockSpec((2, length, 128), lambda h: (0, 0, h)),
            pl.BlockSpec((1, 2 * blocks, 128), lambda h: (h, 0, 0)),
        ],
        out_specs=[
            pl.BlockSpec((1, 128, 256), lambda h: (h, 0, 0)),
            pl.BlockSpec((1, length, 128), lambda h: (h, 0, 0)),
            pl.BlockSpec((1, length, 128), lambda h: (h, 0, 0)),
        ],
        out_shape=[
            jax.ShapeDtypeStruct((heads, 128, 256), F32),
            jax.ShapeDtypeStruct((heads, length, 128), F32),
            jax.ShapeDtypeStruct((heads, length, 128), F32),
        ],
        name="local_phase",
    )(queries, keys, values, small)


def then(earlier, later):
    return add_right(mul(later[:, :128], earlier), later[:, 128:])


def exchange_kernel(
    inner, outer, x_ref, e_ref, got, groups, mine, ready, came,
    send1, recv1, send2, recv2, send3, recv3,
):
    me = lax.axis_index("inner")
    group = lax.axis_index("outer")
    barrier = pltpu.get_barrier_semaphore()
    for d in range(1, inner):
        pl.semaphore_signal(
            barrier, inc=1, device_id=(group, (me + d) % inner),
            device_id_type=pl.DeviceIdType.MESH,
        )
    for d in range(1, outer):
        pl.semaphore_signal(
            barrier, inc=1, device_id=((group + d) % outer, me),
            device_id_type=pl.DeviceIdType.MESH,
        )
    pl.semaphore_wait(barrier, inner + outer - 2)

    first = []
    for d in range(1, inner):
        to = (me + d) % inner
        copy = pltpu.make_async_remote_copy(
            src_ref=x_ref.at[to], dst_ref=got.at[d],
            send_sem=send1.at[d], recv_sem=recv1.at[d],
            device_id=(group, to), device_id_type=pl.DeviceIdType.MESH,
        )
        copy.start()
        first.append(copy)
    got[0] = x_ref[me]
    for copy in first:
        copy.wait()

    before = [None]
    state = got[me]
    for i in range(1, inner + 1):
        before.append(state)
        if i < inner:
            state = then(state, got[(me - i + inner) % inner])
    total = before[inner]
    mine[...] = total

    second = []
    for d in range(1, outer):
        copy = pltpu.make_async_remote_copy(
            src_ref=mine, dst_ref=groups.at[d],
            send_sem=send2.at[d], recv_sem=recv2.at[d],
            device_id=((group + d) % outer, me), device_id_type=pl.DeviceIdType.MESH,
        )
        copy.start()
        second.append(copy)
    groups[0] = total
    for copy in second:
        copy.wait()
    start = jnp.zeros((128, 128), F32)
    for g in range(outer - 1):
        pair = groups[(group - g + outer) % outer]
        moved = mul(pair[:, :128], start) + pair[:, 128:]
        start = jnp.where(g < group, moved, start)

    ready[0] = start
    for i in range(1, inner):
        ready[i] = mul(before[i][:, :128], start) + before[i][:, 128:]
    third = []
    for d in range(1, inner):
        to = (me + d) % inner
        copy = pltpu.make_async_remote_copy(
            src_ref=ready.at[to], dst_ref=came.at[me],
            send_sem=send3.at[d], recv_sem=recv3.at[d],
            device_id=(group, to), device_id_type=pl.DeviceIdType.MESH,
        )
        copy.start()
        third.append(copy)
    e_ref[me] = ready[me]
    for copy in third:
        copy.wait()
    for d in range(1, inner):
        frm = (me + d) % inner
        e_ref[frm] = came[frm]


def exchange(pairs, inner, outer):
    heads = pairs.shape[0]
    vmem = pl.BlockSpec(memory_space=pltpu.VMEM)
    dma = pltpu.SemaphoreType.DMA
    return pl.pallas_call(
        functools.partial(exchange_kernel, inner, outer),
        in_specs=[vmem],
        out_specs=vmem,
        out_shape=jax.ShapeDtypeStruct((heads, 128, 128), F32),
        scratch_shapes=[
            pltpu.VMEM((inner, 128, 256), F32),
            pltpu.VMEM((outer, 128, 256), F32),
            pltpu.VMEM((128, 256), F32),
            pltpu.VMEM((inner, 128, 128), F32),
            pltpu.VMEM((inner, 128, 128), F32),
            dma((inner,)), dma((inner,)),
            dma((outer,)), dma((outer,)),
            dma((inner,)), dma((inner,)),
        ],
        compiler_params=pltpu.CompilerParams(collective_id=0, has_side_effects=True),
        name="exchange",
    )(pairs)


HIGHEST = lax.Precision.HIGHEST


def join(earlier, later):
    moved = jnp.einsum("hde,hef->hdf", later[..., :128], earlier, precision=HIGHEST)
    return jnp.concatenate([moved[..., :128], moved[..., 128:] + later[..., 128:]], -1)


def entering(pairs, axis, begin):
    gathered = lax.all_gather(pairs, axis)

    def one(hop, state):
        return join(state, lax.dynamic_index_in_dim(gathered, hop, 0, False))

    return lax.fori_loop(0, lax.axis_index(axis), one, begin)


def exchange_plain(pairs):
    eye = jnp.concatenate([jnp.eye(128, dtype=F32), jnp.zeros((128, 128), F32)], 1)
    begin = jnp.zeros_like(pairs) + eye
    before = entering(pairs, "inner", begin)
    through = join(before, pairs)
    last = lax.axis_index("inner") == lax.axis_size("inner") - 1
    total = lax.psum(jnp.where(last, through, 0.0), "inner")
    start = entering(total, "outer", begin)
    return join(start, before)[..., 128:]


def finish_kernel(c_ref, b_ref, e_ref, g_ref, o_ref):
    readout = mul(c_ref[0], e_ref[0]) + b_ref[0]
    mean_sq = jnp.mean(readout * readout, 1, keepdims=True)
    o_ref[...] = (readout * lax.rsqrt(mean_sq + 1e-05) * g_ref[...]).astype(BF16)


def finish(carried, base, state, out_gain):
    heads, length, _ = carried.shape
    return pl.pallas_call(
        finish_kernel,
        grid=(heads,),
        in_specs=[
            pl.BlockSpec((1, length, 128), lambda h: (h, 0, 0)),
            pl.BlockSpec((1, length, 128), lambda h: (h, 0, 0)),
            pl.BlockSpec((1, 128, 128), lambda h: (h, 0, 0)),
            pl.BlockSpec((1, 128), lambda h: (0, 0)),
        ],
        out_specs=pl.BlockSpec((length, 128), lambda h: (0, h)),
        out_shape=jax.ShapeDtypeStruct((length, heads * 128), BF16),
        name="finish",
    )(carried, base, state, out_gain.reshape(1, 128))


def per_device(inner, outer, queries, keys, values, betas, log_decay, out_gain):
    heads = betas.shape[1]
    pairs, carried, base = local_phase(queries, keys, values, betas, log_decay)
    if inner == heads:
        state = exchange(pairs, inner, outer)
    else:
        state = exchange_plain(pairs)
    return finish(carried, base, state, out_gain)


def solution(mesh):
    both = ("outer", "inner")
    placed = (P(both, None), P(None, both, None), P(None, both, None), P(None, None, both), P(None, both), P())
    return jax.shard_map(
        functools.partial(per_device, mesh.shape["inner"], mesh.shape["outer"]),
        mesh=mesh,
        in_specs=placed,
        out_specs=P(both, None),
        check_vma=False,
    )
```

time: 692 us -> 94 us (0.14)
  other arithmetic: 324 us -> 0.66 us
  waiting for transfers between devices: 247 us -> 0 us
  Pallas kernels: 0 us -> 91.3 us
  matrix products: 83.6 us -> 0 us
  local copies, waits for them, and re-layouts: 17.3 us -> 1.69 us
  between operations: 13.5 us -> 0.03 us
    another operation x5 -> x0, other arithmetic: 317 us -> none  [the longest x2 316 us: prepare(): lax.linalg.triangular_solve(system, right_side, left_side=True, lower=Tru...]
    all_gather x4 -> x0, waiting for transfers between devices: 168 us -> none  [entering(): gathered = jax.tree.map(lambda a: lax.all_gather(a, axis), part)]
    pallas_call x0 -> x3, Pallas kernels: none -> 91.3 us  [the longest x1 50.2 us: exchange(): pl.pallas_call(functools.partial(exchange_kernel, inner, outer), in_specs...]
    psum x1 -> x0, waiting for transfers between devices: 78.8 us -> none  [spread(): return lax.psum(jnp.where(mine, x, jnp.zeros_like(x)), axis)]
    dot_general x34 -> x0, matrix products: 77 us -> none  [the longest x10 20.4 us: compose(): jnp.einsum('hde,hef->hdf', earlier[1], later[0], precision=HIGHEST)]
  transfers between devices with their start and end apart: 5 -> 0, of which waited for: 5 -> 0; matrix products, arithmetic and copies ran while one was open for 0% -> 0% of each run, Pallas kernels for 0% -> 0%
where the time goes in v1:
time: 94 us; the launch traced here: 93.7 us
  Pallas kernels  91.3 us (97%)
  local copies, waits for them, and re-layouts  1.69 us (2%)
    pallas_call x1, Pallas kernels, exchange(): pl.pallas_call(functools.partial(exchange_kernel, inner, outer), in_specs...  50.2 us
    pallas_call x1, Pallas kernels, local_phase(): pl.pallas_call(functools.partial(local_kernel, blocks), grid=(heads,), in...  34.6 us
    pallas_call x1, Pallas kernels, finish(): pl.pallas_call(finish_kernel, grid=(heads,), in_specs=[pl.BlockSpec((1, l...  6.47 us

profile of v1, /device:TPU:13, one launch (start us, length us, event | category | flops | bytes accessed | tf_op | source)
XLA Modules:
  0.0 93.7 jit_solution(14198843899577591216)
XLA Ops:
  0.0 0.8 reshape.15
  0.8 0.0 copy-start
  0.8 0.1 reshape.16
  0.9 0.6 copy-done
  1.5 0.1 reshape.17
  1.7 0.1 reshape.18
  1.7 0.6 pad_maximum_fusion.1.s_ref
  2.4 34.6 %local_phase.1 = (f32[8,128,256]{2,1,0:T(8,128)}, f32[8,256,128]{2,1,0:T(8,128)}, f32[8,256,128]{2,1,0:T(8,128)}) custom-call(bf16[256,1024]{1,0:T(8,128)(2,1)} %q_ref.1, bf16[2,256,1024]{2,1,0:T(8,128)(2,1)} %k_ref.1, bf16[2,256,1024]{2,1,0:T(8,128)(2,1)} %v_ref.1, f32[8,8,128]{2,1,0:T(8,128)} %pad_maximum_fusion.1.s_ref), custom_call_target="tpu_custom_call" | custom-call | tf_op jit(solution)/shard_map/local_phase/pallas_call | solution.py:141
  36.9 50.2 %exchange.1.e_ref = f32[8,128,128]{2,1,0:T(8,128)} custom-call(f32[8,128,256]{2,1,0:T(8,128)} %get-tuple-element.10.x_ref), custom_call_target="tpu_custom_call" | custom-call | tf_op jit(solution)/shard_map/exchange/pallas_call | solution.py:253
  87.2 6.5 %finish.1 = bf16[256,1024]{1,0:T(8,128)(2,1)} custom-call(f32[8,256,128]{2,1,0:T(8,128)} %get-tuple-element.8.c_ref, f32[8,256,128]{2,1,0:T(8,128)} %get-tuple-element.9.b_ref, f32[8,128,128]{2,1,0:T(8,128)} %exchange.1.e_ref, f32[1,128]{1,0:T(1,128)} %bitcast.7), custom_call_target="tpu_custom_call" | custom-call | tf_op jit(solution)/shard_map/finish/pallas_call | solution.py:309
  (2 shorter events, 0.1 us)
Async XLA Ops:
  0.8 0.7 copy-start

commit v2 on v1

--- a/solution.py
+++ b/solution.py
@@ -48,7 +48,7 @@
     return jnp.concatenate([x[:, :128], x[:, 128:] + y], 1)
 
 
-def local_kernel(blocks, q_ref, k_ref, v_ref, s_ref, x_ref, c_ref, b_ref):
+def masks():
     span = BLOCK_LEN
     size = 2 * span
     row = lax.broadcasted_iota(jnp.int32, (size, size), 0)
@@ -70,14 +70,15 @@
         )
         width *= 2
 
+    return row, col_t, row_t, eye, eye_f, lower, c_mask, r_mask, levels
+
+
+def head_maps(blocks, heads_in, load, emit):
+    span = BLOCK_LEN
+    row, col_t, row_t, eye, eye_f, lower, c_mask, r_mask, levels = masks()
     work = []
-    for n in range(blocks):
-        at = pl.ds(n * span, span)
-        q_b = q_ref[at, :]
-        k_b = jnp.concatenate([k_ref[0, at, :], k_ref[1, at, :]], 0)
-        v_b = jnp.concatenate([v_ref[0, at, :], v_ref[1, at, :]], 0)
-        d_row = s_ref[0, n : n + 1, :]
-        beta_row = s_ref[0, blocks + n : blocks + n + 1, :]
+    for i, n in [(i, n) for i in range(heads_in) for n in range(blocks)]:
+        q_b, k_b, v_b, d_row, beta_row = load(i, n)
         d_col = jnp.sum(jnp.where(eye, d_row, 0.0), 1, keepdims=True)
         beta_col = jnp.sum(jnp.where(eye, beta_row, 0.0), 1, keepdims=True)
         c_col = jnp.sum(jnp.where(c_mask, d_row, 0.0), 1, keepdims=True)
@@ -100,44 +101,65 @@
         part = [mul(jnp.where(mask, w[7], 0.0), t) for w, t in zip(work, inverse)]
         inverse = [t - mul(t, p) for t, p in zip(inverse, part)]
 
-    state = None
+    states = [None] * heads_in
     for n in range(blocks):
-        k_b, v_b, beta_row, c_row, c_col, ki_row, ki_col, low, reach, query = work[n]
-        t = inverse[n] * beta_row
-        written = jnp.concatenate(
-            [mul_left(t * (ki_row * jnp.exp(c_row)), k_b), mul_left(t, v_b)], 1
-        )
-        got = mul(reach, written)
-        reduced, local_out = query - got[:, :128], got[:, 128:]
-        last = c_col[span - 1 : span, :]
-        tail = jnp.exp(last - c_col) * ki_col
-        wh, wl = split(written * tail)
-        k_t = jnp.transpose(k_b.astype(F32)).astype(BF16)
-        made = dot(jnp.concatenate([k_t, k_t], 1), jnp.concatenate([wh, wl], 0))
-        trans = jnp.exp(last) * eye_f - made[:, :128]
-        inject = made[:, 128:]
-        at = pl.ds(n * span, span)
-        if state is None:
-            c_ref[0, at, :] = reduced
-            b_ref[0, at, :] = local_out
-            state = jnp.concatenate([trans, inject], 1)
-        else:
-            read = mul(reduced, state)
-            c_ref[0, at, :] = read[:, :128]
-            b_ref[0, at, :] = read[:, 128:] + local_out
-            state = add_right(mul(trans, state), inject)
-    x_ref[0] = state
-
-
-def local_phase(queries, keys, values, betas, log_decay):
-    length = queries.shape[0]
-    heads = betas.shape[1]
+        for i in range(heads_in):
+            state = states[i]
+            k_b, v_b, beta_row, c_row, c_col, ki_row, ki_col, low, reach, query = work[i * blocks + n]
+            t = inverse[i * blocks + n] * beta_row
+            written = jnp.concatenate(
+                [mul_left(t * (ki_row * jnp.exp(c_row)), k_b), mul_left(t, v_b)], 1
+            )
+            got = mul(reach, written)
+            reduced, local_out = query - got[:, :128], got[:, 128:]
+            last = c_col[span - 1 : span, :]
+            tail = jnp.exp(last - c_col) * ki_col
+            wh, wl = split(written * tail)
+            k_t = jnp.transpose(k_b.astype(F32)).astype(BF16)
+            made = dot(jnp.concatenate([k_t, k_t], 1), jnp.concatenate([wh, wl], 0))
+            trans = jnp.exp(last) * eye_f - made[:, :128]
+            inject = made[:, 128:]
+            if state is None:
+                emit(i, n, reduced, local_out)
+                states[i] = jnp.concatenate([trans, inject], 1)
+            else:
+                read = mul(reduced, state)
+                emit(i, n, read[:, :128], read[:, 128:] + local_out)
+                states[i] = add_right(mul(trans, state), inject)
+    return states
+
+
+def local_kernel(blocks, q_ref, k_ref, v_ref, s_ref, x_ref, c_ref, b_ref):
+    def load(i, n):
+        at = pl.ds(n * BLOCK_LEN, BLOCK_LEN)
+        k_b = jnp.concatenate([k_ref[0, at, :], k_ref[1, at, :]], 0)
+        v_b = jnp.concatenate([v_ref[0, at, :], v_ref[1, at, :]], 0)
+        return q_ref[at, :], k_b, v_b, s_ref[0, n : n + 1, :], s_ref[0, blocks + n : blocks + n + 1, :]
+
+    def emit(i, n, carried, base):
+        at = pl.ds(n * BLOCK_LEN, BLOCK_LEN)
+        c_ref[0, at, :] = carried
+        b_ref[0, at, :] = base
+
+    x_ref[0] = head_maps(blocks, 1, load, emit)[0]
+
+
+def small_rows(betas, log_decay):
+    heads, length = log_decay.shape
     blocks = length // BLOCK_LEN
     beta = betas.reshape(2, heads, blocks, BLOCK_LEN).transpose(1, 2, 0, 3)
     beta = beta.reshape(heads, blocks, 2 * BLOCK_LEN)
     decay = log_decay.reshape(heads, blocks, 1, BLOCK_LEN)
     decay = jnp.concatenate([decay, decay], 2).reshape(heads, blocks, 2 * BLOCK_LEN)
     small = jnp.concatenate([decay, beta], 1)
+    return small
+
+
+def local_phase(queries, keys, values, betas, log_decay):
+    length = queries.shape[0]
+    heads = betas.shape[1]
+    blocks = length // BLOCK_LEN
+    small = small_rows(betas, log_decay)
     return pl.pallas_call(
         functools.partial(local_kernel, blocks),
         grid=(heads,),
@@ -165,109 +187,187 @@
     return add_right(mul(later[:, :128], earlier), later[:, 128:])
 
 
-def exchange_kernel(
-    inner, outer, x_ref, e_ref, got, groups, mine, ready, came,
+TOGETHER = 2
+
+
+def normed(carried, base, state, gain):
+    readout = mul(carried, state) + base
+    mean_sq = jnp.mean(readout * readout, 1, keepdims=True)
+    return (readout * lax.rsqrt(mean_sq + 1e-05) * gain).astype(BF16)
+
+
+def whole_kernel(
+    inner, outer, q_ref, k_ref, v_ref, s_ref, g_ref, o_ref,
+    sent, got, groups, mine, ready, came, c_buf, b_buf,
     send1, recv1, send2, recv2, send3, recv3,
 ):
+    mesh_id = pl.DeviceIdType.MESH
+    length = q_ref.shape[0]
+    blocks = length // BLOCK_LEN
     me = lax.axis_index("inner")
     group = lax.axis_index("outer")
+    groups[...] = jnp.zeros_like(groups)
     barrier = pltpu.get_barrier_semaphore()
     for d in range(1, inner):
-        pl.semaphore_signal(
-            barrier, inc=1, device_id=(group, (me + d) % inner),
-            device_id_type=pl.DeviceIdType.MESH,
+        pl.semaphore_signal(barrier, inc=1, device_id=(group, (me + d) % inner), device_id_type=mesh_id)
+    for d in range(1, outer):
+        pl.semaphore_signal(barrier, inc=1, device_id=((group + d) % outer, me), device_id_type=mesh_id)
+    pl.semaphore_wait(barrier, inner + outer - 2)
+
+    def map_copy(slot):
+        to = (me + slot) % inner
+        return pltpu.make_async_remote_copy(
+            src_ref=sent.at[slot], dst_ref=got.at[slot],
+            send_sem=send1.at[slot], recv_sem=recv1.at[slot],
+            device_id=(group, to), device_id_type=mesh_id,
         )
-    for d in range(1, outer):
-        pl.semaphore_signal(
-            barrier, inc=1, device_id=((group + d) % outer, me),
-            device_id_type=pl.DeviceIdType.MESH,
-        )
-    pl.semaphore_wait(barrier, inner + outer - 2)
-
-    first = []
-    for d in range(1, inner):
-        to = (me + d) % inner
-        copy = pltpu.make_async_remote_copy(
-            src_ref=x_ref.at[to], dst_ref=got.at[d],
-            send_sem=send1.at[d], recv_sem=recv1.at[d],
-            device_id=(group, to), device_id_type=pl.DeviceIdType.MESH,
-        )
-        copy.start()
-        first.append(copy)
-    got[0] = x_ref[me]
-    for copy in first:
-        copy.wait()
-
-    before = [None]
-    state = got[me]
-    for i in range(1, inner + 1):
-        before.append(state)
-        if i < inner:
-            state = then(state, got[(me - i + inner) % inner])
-    total = before[inner]
-    mine[...] = total
-
-    second = []
-    for d in range(1, outer):
-        copy = pltpu.make_async_remote_copy(
+
+    def step(turn, carry):
+        places = [turn * TOGETHER + i + 1 for i in range(TOGETHER)]
+        heads = [(me + p) % inner for p in places]
+
+        def load(i, n):
+            at = pl.ds(n * BLOCK_LEN, BLOCK_LEN)
+            lanes = pl.ds(pl.multiple_of(heads[i] * 128, 128), 128)
+            k_b = jnp.concatenate([k_ref[0, at, lanes], k_ref[1, at, lanes]], 0)
+            v_b = jnp.concatenate([v_ref[0, at, lanes], v_ref[1, at, lanes]], 0)
+            rows = s_ref[heads[i]]
+            return q_ref[at, lanes], k_b, v_b, rows[n : n + 1], rows[blocks + n : blocks + n + 1]
+
+        def emit(i, n, carried, base):
+            at = pl.ds(n * BLOCK_LEN, BLOCK_LEN)
+            c_buf[heads[i], at, :] = carried
+            b_buf[heads[i], at, :] = base
+
+        states = head_maps(blocks, TOGETHER, load, emit)
+        for i in range(TOGETHER):
+            sent[places[i]] = states[i]
+            if i < TOGETHER - 1:
+                map_copy(places[i]).start()
+            else:
+
+                @pl.when(places[i] < inner)
+                def _():
+                    map_copy(places[i]).start()
+
+        return carry
+
+    lax.fori_loop(0, inner // TOGETHER, step, 0)
+    got[0] = sent[inner]
+    for slot in range(1, inner):
+        map_copy(slot).wait()
+
+    maps = [got[(me - i + inner) % inner] for i in range(inner)]
+
+    def tree(parts):
+        if len(parts) == 1:
+            return parts
+        half = len(parts) // 2
+        pairs = [then(parts[2 * i], parts[2 * i + 1]) for i in range(half)]
+        return pairs
+
+    level = maps
+    levels = [maps]
+    while len(level) > 1:
+        level = tree(level)
+        levels.append(level)
+    mine[...] = level[0]
+
+    def group_copy(d):
+        return pltpu.make_async_remote_copy(
             src_ref=mine, dst_ref=groups.at[d],
             send_sem=send2.at[d], recv_sem=recv2.at[d],
-            device_id=((group + d) % outer, me), device_id_type=pl.DeviceIdType.MESH,
+            device_id=((group + d) % outer, me), device_id_type=mesh_id,
         )
-        copy.start()
-        second.append(copy)
-    groups[0] = total
-    for copy in second:
-        copy.wait()
+
+    for d in range(1, outer):
+
+        @pl.when(group + d < outer)
+        def _():
+            group_copy(d).start()
+
+    before = {}
+    for i in range(1, inner):
+        low = i & -i
+        height = low.bit_length() - 1
+        part = levels[height][(i - low) >> height]
+        before[i] = part if i == low else then(before[i - low], part)
+    left = wide(jnp.concatenate([before[i][:, :128] for i in range(1, inner)], 0))
+    right = jnp.concatenate([before[i][:, 128:] for i in range(1, inner)], 0)
+
+    for d in range(1, outer):
+
+        @pl.when(group + d < outer)
+        def _():
+            group_copy(d).wait_send()
+
+        @pl.when(group - d >= 0)
+        def _():
+            group_copy(d).wait_recv()
+
     start = jnp.zeros((128, 128), F32)
     for g in range(outer - 1):
         pair = groups[(group - g + outer) % outer]
         moved = mul(pair[:, :128], start) + pair[:, 128:]
         start = jnp.where(g < group, moved, start)
 
+    sh, sl = split(start)
+    row = jnp.concatenate([sh, sl], 1)
+    both = dot(left, jnp.concatenate([row, row], 0))
     ready[0] = start
-    for i in range(1, inner):
-        ready[i] = mul(before[i][:, :128], start) + before[i][:, 128:]
-    third = []
+    ready[pl.ds(1, inner - 1)] = (both[:, :128] + both[:, 128:] + right).reshape(inner - 1, 128, 128)
+
+    def back_copy(d):
+        to = (me + d) % inner
+        return pltpu.make_async_remote_copy(
+            src_ref=ready.at[to], dst_ref=came.at[d],
+            send_sem=send3.at[d], recv_sem=recv3.at[d],
+            device_id=(group, to), device_id_type=mesh_id,
+        )
+
     for d in range(1, inner):
-        to = (me + d) % inner
-        copy = pltpu.make_async_remote_copy(
-            src_ref=ready.at[to], dst_ref=came.at[me],
-            send_sem=send3.at[d], recv_sem=recv3.at[d],
-            device_id=(group, to), device_id_type=pl.DeviceIdType.MESH,
-        )
-        copy.start()
-        third.append(copy)
-    e_ref[me] = ready[me]
-    for copy in third:
-        copy.wait()
-    for d in range(1, inner):
-        frm = (me + d) % inner
-        e_ref[frm] = came[frm]
-
-
-def exchange(pairs, inner, outer):
-    heads = pairs.shape[0]
+        back_copy(d).start()
+    came[0] = ready[me]
+
+    def out(d):
+        head = (me - d + inner) % inner
+        lanes = pl.ds(pl.multiple_of(head * 128, 128), 128)
+        o_ref[:, lanes] = normed(c_buf[head], b_buf[head], came[d], g_ref[...])
+
+    out(0)
+    for first in range(1, inner, 2):
+        some = range(first, min(first + 2, inner))
+        for d in some:
+            back_copy(d).wait()
+        for d in some:
+            out(d)
+
+
+def whole(inner, outer, queries, keys, values, betas, log_decay, out_gain):
+    length, width = queries.shape
     vmem = pl.BlockSpec(memory_space=pltpu.VMEM)
     dma = pltpu.SemaphoreType.DMA
     return pl.pallas_call(
-        functools.partial(exchange_kernel, inner, outer),
-        in_specs=[vmem],
+        functools.partial(whole_kernel, inner, outer),
+        in_specs=[vmem] * 5,
         out_specs=vmem,
-        out_shape=jax.ShapeDtypeStruct((heads, 128, 128), F32),
+        out_shape=jax.ShapeDtypeStruct((length, width), BF16),
         scratch_shapes=[
+            pltpu.VMEM((inner + 1, 128, 256), F32),
             pltpu.VMEM((inner, 128, 256), F32),
             pltpu.VMEM((outer, 128, 256), F32),
             pltpu.VMEM((128, 256), F32),
             pltpu.VMEM((inner, 128, 128), F32),
             pltpu.VMEM((inner, 128, 128), F32),
+            pltpu.VMEM((inner, length, 128), F32),
+            pltpu.VMEM((inner, length, 128), F32),
             dma((inner,)), dma((inner,)),
             dma((outer,)), dma((outer,)),
             dma((inner,)), dma((inner,)),
         ],
         compiler_params=pltpu.CompilerParams(collective_id=0, has_side_effects=True),
-        name="exchange",
-    )(pairs)
+        name="whole",
+    )(queries, keys, values, small_rows(betas, log_decay), out_gain.reshape(1, 128))
 
 
 HIGHEST = lax.Precision.HIGHEST
@@ -323,12 +423,10 @@
 
 def per_device(inner, outer, queries, keys, values, betas, log_decay, out_gain):
     heads = betas.shape[1]
+    if inner == heads:
+        return whole(inner, outer, queries, keys, values, betas, log_decay, out_gain)
     pairs, carried, base = local_phase(queries, keys, values, betas, log_decay)
-    if inner == heads:
-        state = exchange(pairs, inner, outer)
-    else:
-        state = exchange_plain(pairs)
-    return finish(carried, base, state, out_gain)
+    return finish(carried, base, exchange_plain(pairs), out_gain)
 
 
 def solution(mesh):

time: 94 us -> 62.5 us (0.66)
  the two profiles are of different devices: /device:TPU:13 before, /device:TPU:31 now
where the time goes in v2:
time: 62.5 us; the launch traced here: 62.2 us
  Pallas kernels  58 us (93%)
  local copies, waits for them, and re-layouts  3.56 us (6%)
  other arithmetic  0.66 us (1%)
    pallas_call x1, Pallas kernels, whole(): pl.pallas_call(functools.partial(whole_kernel, inner, outer), in_specs=[v...  58 us
    unnamed x3, local copies, waits for them, and re-layouts  2.49 us

profile of v2, /device:TPU:31, one launch (start us, length us, event | category | flops | bytes accessed | tf_op | source)
XLA Modules:
  0.0 62.2 jit_solution(17786802955514713765)
XLA Ops:
  0.0 0.8 %reshape.15 = f32[8,4,1,64]{3,1,0,2:T(4,128)S(1)} reshape(f32[8,256]{1,0:T(8,128)} %param.10) | data formatting | bytes 16384 | tf_op jit(solution)/shard_map/reshape | solution.py:152
  0.8 0.0 copy-start
  0.8 0.1 reshape.16
  0.9 0.6 copy-done
  1.5 0.1 reshape.17
  1.7 0.1 reshape.18
  1.7 0.6 %pad_maximum_fusion.1.s_ref = f32[8,8,128]{2,1,0:T(8,128)} fusion(f32[8,4,128]{2,1,0:T(4,128)S(1)} %reshape.18, f32[8,4,128]{2,1,0:T(4,128)S(1)} %reshape.16), kind=kLoop, calls=%fused_computation.1 | loop fusion | flops 8192 | bytes 65536 | tf_op jit(solution)/shard_map/concatenate | solution.py:154
  2.4 58.0 %whole.1 = bf16[256,1024]{1,0:T(8,128)(2,1)} custom-call(bf16[256,1024]{1,0:T(8,128)(2,1)} %q_ref.1, bf16[2,256,1024]{2,1,0:T(8,128)(2,1)} %k_ref.1, bf16[2,256,1024]{2,1,0:T(8,128)(2,1)} %v_ref.1, f32[8,8,128]{2,1,0:T(8,128)} %pad_maximum_fusion.1.s_ref, f32[1,128]{1,0:T(1,128)} %bitcast.7), custom_call_target="tpu_custom_call" | custom-call | tf_op jit(solution)/shard_map/whole/pallas_call | solution.py:350
  60.3 1.9 %copy.13 = bf16[256,1024]{1,0:T(8,128)(2,1)} copy(bf16[256,1024]{1,0:T(8,128)(2,1)} %whole.1) | data formatting | bytes 1048576
  (2 shorter events, 0.1 us)
Async XLA Ops:
  0.8 0.7 %copy-start = (f32[2,8,256]{2,1,0:T(8,128)S(1)}, f32[2,8,256]{2,1,0:T(8,128)}, u32[]{:S(2)}) copy-start(f32[2,8,256]{2,1,0:T(8,128)} %param.9) | copy-start | bytes 49156

commit v3 on v2

--- a/solution.py
+++ b/solution.py
@@ -53,8 +53,10 @@
     size = 2 * span
     row = lax.broadcasted_iota(jnp.int32, (size, size), 0)
     col = lax.broadcasted_iota(jnp.int32, (size, size), 1)
-    row_t, col_t = row % span, col % span
-    row_rank, col_rank = 2 * row_t + row // span, 2 * col_t + col // span
+    row_t, col_t = row & (span - 1), col & (span - 1)
+    row_rank = 2 * row_t + (row >= span).astype(jnp.int32)
+    col_rank = 2 * col_t + (col >= span).astype(jnp.int32)
+    differ = row_rank ^ col_rank
     eye = row == col
     eye_f = eye.astype(F32)
     lower = row_rank > col_rank
@@ -64,9 +66,7 @@
     width = 1
     while width < size:
         levels.append(
-            (row_rank // (2 * width) == col_rank // (2 * width))
-            & (row_rank // width != col_rank // width)
-            & lower
+            (differ >= width) & (differ < 2 * width) & lower
         )
         width *= 2
 
@@ -187,9 +187,6 @@
     return add_right(mul(later[:, :128], earlier), later[:, 128:])
 
 
-TOGETHER = 2
-
-
 def normed(carried, base, state, gain):
     readout = mul(carried, state) + base
     mean_sq = jnp.mean(readout * readout, 1, keepdims=True)
@@ -198,33 +195,52 @@
 
 def whole_kernel(
     inner, outer, q_ref, k_ref, v_ref, s_ref, g_ref, o_ref,
-    sent, got, groups, mine, ready, came, c_buf, b_buf,
-    send1, recv1, send2, recv2, send3, recv3,
+    away, near, own, even_map, sent, got, groups, mine, ready, came, aside, beside, c_buf, b_buf,
+    send0, recv0, send1, recv1, send2, recv2, send3, recv3, send4, recv4,
 ):
     mesh_id = pl.DeviceIdType.MESH
     length = q_ref.shape[0]
     blocks = length // BLOCK_LEN
     me = lax.axis_index("inner")
     group = lax.axis_index("outer")
+    core, chip, chips = me % 2, me // 2, inner // 2
+    partner = chip * 2 + 1 - core
     groups[...] = jnp.zeros_like(groups)
     barrier = pltpu.get_barrier_semaphore()
-    for d in range(1, inner):
-        pl.semaphore_signal(barrier, inc=1, device_id=(group, (me + d) % inner), device_id_type=mesh_id)
+    for d in range(1, chips):
+        pl.semaphore_signal(
+            barrier, inc=1, device_id=(group, (chip + d) % chips * 2 + core), device_id_type=mesh_id
+        )
+    pl.semaphore_signal(barrier, inc=1, device_id=(group, partner), device_id_type=mesh_id)
     for d in range(1, outer):
         pl.semaphore_signal(barrier, inc=1, device_id=((group + d) % outer, me), device_id_type=mesh_id)
-    pl.semaphore_wait(barrier, inner + outer - 2)
-
-    def map_copy(slot):
-        to = (me + slot) % inner
+    pl.semaphore_wait(barrier, chips + outer - 1)
+
+    def near_copy(turn):
         return pltpu.make_async_remote_copy(
-            src_ref=sent.at[slot], dst_ref=got.at[slot],
-            send_sem=send1.at[slot], recv_sem=recv1.at[slot],
-            device_id=(group, to), device_id_type=mesh_id,
-        )
+            src_ref=away.at[turn], dst_ref=near.at[turn],
+            send_sem=send0.at[turn], recv_sem=recv0.at[turn],
+            device_id=(group, partner), device_id_type=mesh_id,
+        )
+
+    def map_copy(d):
+        return pltpu.make_async_remote_copy(
+            src_ref=sent.at[d], dst_ref=got.at[d],
+            send_sem=send1.at[d], recv_sem=recv1.at[d],
+            device_id=(group, (chip + d) % chips * 2 + core), device_id_type=mesh_id,
+        )
+
+    def chip_map(turn):
+        near_copy(turn).wait()
+        here, there = own[turn], near[turn]
+        even = jnp.where(core == 0, here, there)
+        odd = jnp.where(core == 0, there, here)
+        even_map[turn] = even
+        return then(even, odd)
 
     def step(turn, carry):
-        places = [turn * TOGETHER + i + 1 for i in range(TOGETHER)]
-        heads = [(me + p) % inner for p in places]
+        far = (chip + turn + 1) % chips * 2
+        heads = [far + core, far + 1 - core]
 
         def load(i, n):
             at = pl.ds(n * BLOCK_LEN, BLOCK_LEN)
@@ -239,25 +255,24 @@
             c_buf[heads[i], at, :] = carried
             b_buf[heads[i], at, :] = base
 
-        states = head_maps(blocks, TOGETHER, load, emit)
-        for i in range(TOGETHER):
-            sent[places[i]] = states[i]
-            if i < TOGETHER - 1:
-                map_copy(places[i]).start()
-            else:
-
-                @pl.when(places[i] < inner)
-                def _():
-                    map_copy(places[i]).start()
+        states = head_maps(blocks, 2, load, emit)
+        away[turn] = states[1]
+        near_copy(turn).start()
+        own[turn] = states[0]
+
+        @pl.when(turn > 0)
+        def _():
+            sent[turn] = chip_map(turn - 1)
+            map_copy(turn).start()
 
         return carry
 
-    lax.fori_loop(0, inner // TOGETHER, step, 0)
-    got[0] = sent[inner]
-    for slot in range(1, inner):
-        map_copy(slot).wait()
-
-    maps = [got[(me - i + inner) % inner] for i in range(inner)]
+    lax.fori_loop(0, chips, step, 0)
+    got[0] = chip_map(chips - 1)
+    for d in range(1, chips):
+        map_copy(d).wait()
+
+    maps = [got[(chip - i + chips) % chips] for i in range(chips)]
 
     def tree(parts):
         if len(parts) == 1:
@@ -287,13 +302,13 @@
             group_copy(d).start()
 
     before = {}
-    for i in range(1, inner):
+    for i in range(1, chips):
         low = i & -i
         height = low.bit_length() - 1
         part = levels[height][(i - low) >> height]
         before[i] = part if i == low else then(before[i - low], part)
-    left = wide(jnp.concatenate([before[i][:, :128] for i in range(1, inner)], 0))
-    right = jnp.concatenate([before[i][:, 128:] for i in range(1, inner)], 0)
+    left = wide(jnp.concatenate([before[i][:, :128] for i in range(1, chips)], 0))
+    right = jnp.concatenate([before[i][:, 128:] for i in range(1, chips)], 0)
 
     for d in range(1, outer):
 
@@ -315,32 +330,47 @@
     row = jnp.concatenate([sh, sl], 1)
     both = dot(left, jnp.concatenate([row, row], 0))
     ready[0] = start
-    ready[pl.ds(1, inner - 1)] = (both[:, :128] + both[:, 128:] + right).reshape(inner - 1, 128, 128)
+    ready[pl.ds(1, chips - 1)] = (both[:, :128] + both[:, 128:] + right).reshape(chips - 1, 128, 128)
 
     def back_copy(d):
-        to = (me + d) % inner
+        to = (chip + d) % chips
         return pltpu.make_async_remote_copy(
             src_ref=ready.at[to], dst_ref=came.at[d],
             send_sem=send3.at[d], recv_sem=recv3.at[d],
-            device_id=(group, to), device_id_type=mesh_id,
-        )
-
-    for d in range(1, inner):
+            device_id=(group, to * 2 + core), device_id_type=mesh_id,
+        )
+
+    def side_copy(d):
+        return pltpu.make_async_remote_copy(
+            src_ref=aside.at[d], dst_ref=beside.at[d],
+            send_sem=send4.at[d], recv_sem=recv4.at[d],
+            device_id=(group, partner), device_id_type=mesh_id,
+        )
+
+    for d in range(1, chips):
         back_copy(d).start()
-    came[0] = ready[me]
-
-    def out(d):
-        head = (me - d + inner) % inner
+
+    def out(head, state):
         lanes = pl.ds(pl.multiple_of(head * 128, 128), 128)
-        o_ref[:, lanes] = normed(c_buf[head], b_buf[head], came[d], g_ref[...])
-
-    out(0)
-    for first in range(1, inner, 2):
-        some = range(first, min(first + 2, inner))
-        for d in some:
+        o_ref[:, lanes] = normed(c_buf[head], b_buf[head], state, g_ref[...])
+
+    for d in range(chips):
+        if d:
             back_copy(d).wait()
-        for d in some:
-            out(d)
+            enter = came[d]
+        else:
+            enter = ready[chip]
+        pair = even_map[chips - 1 - d]
+        after = mul(pair[:, :128], enter) + pair[:, 128:]
+        aside[d] = jnp.where(core == 0, after, enter)
+        side_copy(d).start()
+        far = (chip - d + chips) % chips * 2
+        out(far + core, jnp.where(core == 0, enter, after))
+        if d:
+            side_copy(d - 1).wait()
+            out((chip - d + 1 + chips) % chips * 2 + 1 - core, beside[d - 1])
+    side_copy(chips - 1).wait()
+    out((chip + 1) % chips * 2 + 1 - core, beside[chips - 1])
 
 
 def whole(inner, outer, queries, keys, values, betas, log_decay, out_gain):
@@ -353,17 +383,14 @@
         out_specs=vmem,
         out_shape=jax.ShapeDtypeStruct((length, width), BF16),
         scratch_shapes=[
-            pltpu.VMEM((inner + 1, 128, 256), F32),
-            pltpu.VMEM((inner, 128, 256), F32),
+            *[pltpu.VMEM((inner // 2, 128, 256), F32)] * 6,
             pltpu.VMEM((outer, 128, 256), F32),
             pltpu.VMEM((128, 256), F32),
-            pltpu.VMEM((inner, 128, 128), F32),
-            pltpu.VMEM((inner, 128, 128), F32),
-            pltpu.VMEM((inner, length, 128), F32),
-            pltpu.VMEM((inner, length, 128), F32),
-            dma((inner,)), dma((inner,)),
-            dma((outer,)), dma((outer,)),
-            dma((inner,)), dma((inner,)),
+            *[pltpu.VMEM((inner // 2, 128, 128), F32)] * 4,
+            *[pltpu.VMEM((inner, length, 128), F32)] * 2,
+            *[dma((inner // 2,))] * 4,
+            *[dma((outer,))] * 2,
+            *[dma((inner // 2,))] * 4,
         ],
         compiler_params=pltpu.CompilerParams(collective_id=0, has_side_effects=True),
         name="whole",

time: 62.5 us -> 55.4 us (0.89)
  the two profiles are of different devices: /device:TPU:31 before, /device:TPU:13 now
where the time goes in v3:
time: 55.4 us; the launch traced here: 54.6 us
  Pallas kernels  50.3 us (91%)
  local copies, waits for them, and re-layouts  3.56 us (6%)
  other arithmetic  0.66 us (1%)
    pallas_call x1, Pallas kernels, whole(): pl.pallas_call(functools.partial(whole_kernel, inner, outer), in_specs=[v...  50.3 us
    unnamed x3, local copies, waits for them, and re-layouts  2.49 us

profile of v3, /device:TPU:13, one launch (start us, length us, event | category | flops | bytes accessed | tf_op | source)
XLA Modules:
  0.0 54.6 jit_solution(11688194237282795003)
XLA Ops:
  0.0 0.8 %reshape.15 = f32[8,4,1,64]{3,1,0,2:T(4,128)S(1)} reshape(f32[8,256]{1,0:T(8,128)} %param.10) | data formatting | bytes 16384 | tf_op jit(solution)/shard_map/reshape | solution.py:152
  0.8 0.0 copy-start
  0.8 0.1 reshape.16
  0.9 0.6 %copy-done = f32[2,8,256]{2,1,0:T(8,128)S(1)} copy-done((f32[2,8,256]{2,1,0:T(8,128)S(1)}, f32[2,8,256]{2,1,0:T(8,128)}, u32[]{:S(2)}) %copy-start) | copy-done | bytes 16408
  1.5 0.1 reshape.17
  1.7 0.1 reshape.18
  1.7 0.6 %pad_maximum_fusion.1.s_ref = f32[8,8,128]{2,1,0:T(8,128)} fusion(f32[8,4,128]{2,1,0:T(4,128)S(1)} %reshape.18, f32[8,4,128]{2,1,0:T(4,128)S(1)} %reshape.16), kind=kLoop, calls=%fused_computation.1 | loop fusion | flops 8192 | bytes 65536 | tf_op jit(solution)/shard_map/concatenate | solution.py:154
  2.4 50.3 %whole.1 = bf16[256,1024]{1,0:T(8,128)(2,1)} custom-call(bf16[256,1024]{1,0:T(8,128)(2,1)} %q_ref.1, bf16[2,256,1024]{2,1,0:T(8,128)(2,1)} %k_ref.1, bf16[2,256,1024]{2,1,0:T(8,128)(2,1)} %v_ref.1, f32[8,8,128]{2,1,0:T(8,128)} %pad_maximum_fusion.1.s_ref, f32[1,128]{1,0:T(1,128)} %bitcast.7), custom_call_target="tpu_custom_call" | custom-call | tf_op jit(solution)/shard_map/whole/pallas_call | solution.py:380
  52.7 1.9 %copy.13 = bf16[256,1024]{1,0:T(8,128)(2,1)} copy(bf16[256,1024]{1,0:T(8,128)(2,1)} %whole.1) | data formatting | bytes 1048576
  (2 shorter events, 0.1 us)
Async XLA Ops:
  0.8 0.7 %copy-start = (f32[2,8,256]{2,1,0:T(8,128)S(1)}, f32[2,8,256]{2,1,0:T(8,128)}, u32[]{:S(2)}) copy-start(f32[2,8,256]{2,1,0:T(8,128)} %param.9) | copy-start | bytes 49156
